TPU v7x, 512 devices: a whole 4x8x8 slice. The times are simulated.
512 devices in a mesh: lat: 32 (over x, z), lon: 16 (over y, core).
Axes of the slice: x: 4, y: 8, z: 8, core: 2. Of those that a mesh axis runs over, the one named last changes fastest.
Arguments:
- state: float32 [256, 1440, 256], P('lat', 'lon'), may hold values from -6 to 6
- filter_flag: int32 [256], P('lat'), may hold values from 0 to 1, as said below
- cutoff: int32 [256], P('lat'), may hold values from 2 to 179
Outputs:
- state_new: float32 [256, 1440, 256], P('lat', 'lon')
Inputs may be any that keep to these rules, and one draw needn't show every extreme that they name: `filter_flag`: row j is flagged exactly when j < S or j >= 128 + S, for one S between 32 and 96.
All inputs are finite; a program needn't handle non-finite values.
Results may differ from a plain program's by a relative error of at most 0.000057.
Values sent between devices are 32-bit elements; how exact they have to be, the bound alone decides.
A program may use at most 64 MiB of HBM per device.

v0:
```python
import functools
import math

import jax
import jax.numpy as jnp
import numpy as np
from jax import lax
from jax.experimental import pallas as pl
from jax.experimental.pallas import tpu as pltpu
from jax.sharding import PartitionSpec as P

MESH = pl.DeviceIdType.MESH
PARTS = 16
LANES = 128
OPEN_CUT = 4096.0
PACKED = 72


def split_table(table):
    high = np.asarray(table, dtype=jnp.bfloat16)
    low = np.asarray(table - high.astype(np.float64), dtype=jnp.bfloat16)
    return high, low


def dft_tables(nlon, width, wide):
    points = np.full(wide, -10**6)
    points[:width] = np.arange(width)
    points[width] = width
    points[wide - 1] = -1
    used = points > -10**6
    forward = np.zeros((8, 2 * wide, 2 * wide))
    inverse = np.zeros((8, 2 * wide, 2 * wide))
    sines = np.zeros((8, wide))
    for group in range(8):
        for row in range(wide):
            if group:
                if row >= width:
                    continue
                wave = group + PARTS * row
                weight = 2.0 / nlon
            else:
                half = width // 2 + 1
                if row < half:
                    wave = PARTS * row
                elif row < width + 1:
                    wave = 8 + PARTS * (row - half)
                else:
                    continue
                weight = (1.0 if wave in (0, nlon // 2) else 2.0) / nlon
            phase = np.where(used, (points * wave) % nlon, 0) * (2.0 * math.pi / nlon)
            cos_vals = np.where(used, np.cos(phase), 0.0)
            sin_vals = np.where(used, np.sin(phase), 0.0)
            inner = np.arange(wide) < width
            if group:
                forward[group, row, :wide] = cos_vals
                forward[group, row, wide:] = -sin_vals
                forward[group, wide + row, :wide] = -sin_vals
                forward[group, wide + row, wide:] = -cos_vals
                inverse[group, :wide, row] = weight * cos_vals * inner
                inverse[group, :wide, wide + row] = -weight * sin_vals * inner
                inverse[group, wide:, row] = weight * sin_vals * inner
                inverse[group, wide:, wide + row] = weight * cos_vals * inner
            else:
                base = 0 if row < half else wide
                part = slice(base, base + wide)
                forward[0, row, part] = cos_vals
                forward[0, wide + row, part] = -sin_vals
                inverse[0, part, row] = weight * cos_vals * inner
                inverse[0, part, wide + row] = -weight * sin_vals * inner
            sines[group, row] = math.sin(2.0 * math.pi * wave / nlon)
    waves = np.ascontiguousarray(np.broadcast_to(sines.astype(np.float32)[..., None], sines.shape + (LANES,)))
    return split_table(forward) + split_table(inverse) + (waves,)


def coef_table(nlat, bands):
    rows = nlat // bands
    index = np.arange(-1, nlat + 1).astype(np.float32)
    angle = np.float32(-0.5 * math.pi) + (index + np.float32(0.5)) * np.float32(math.pi) / np.float32(nlat)
    cosine = np.cos(angle.astype(np.float64)).astype(np.float32).astype(np.float64)
    flux = cosine.copy()
    flux[0] = 0.0
    flux[-1] = 0.0
    table = np.zeros((bands, 16, LANES))
    for band in range(bands):
        at = band * rows + 1
        for row in range(rows):
            table[band, row] = 0.015 / cosine[at + row]
        for pair in range(rows // 2):
            even = at + 2 * pair
            odd = even + 1
            lane = np.zeros(8)
            lane[0] = 0.03 / cosine[even]
            lane[1] = 0.03 / cosine[odd]
            lane[4] = -0.015 * flux[odd] / cosine[even]
            lane[5] = 0.015 * flux[even] / cosine[odd]
            lane[6] = 0.015 * flux[even - 1] / cosine[even]
            lane[7] = -0.015 * flux[odd + 1] / cosine[odd]
            table[band, 8 + pair] = np.repeat(lane, 16)
    return table.astype(np.float32)


def wave_sum(terms):
    total = None
    for factor, value in terms:
        if abs(factor) < 1e-9:
            continue
        if abs(abs(factor) - 1.0) < 1e-9:
            if total is None:
                total = value if factor > 0 else -value
            else:
                total = total + value if factor > 0 else total - value
        else:
            part = value * np.float32(factor)
            total = part if total is None else total + part
    return total


def half_dft(even_in, odd_in):
    unit = 2.0 * math.pi / PARTS
    sums = [even_in[0] + even_in[8]] + [even_in[a] + even_in[8 - a] for a in (1, 2, 3)] + [even_in[4]]
    diffs = [even_in[0] - even_in[8]] + [even_in[a] - even_in[8 - a] for a in (1, 2, 3)]
    odd_sums = [None] + [odd_in[a] + odd_in[8 - a] for a in (1, 2, 3)] + [odd_in[4]]
    odd_diffs = [None] + [odd_in[a] - odd_in[8 - a] for a in (1, 2, 3)]
    cos_out = []
    sin_out = []
    for k in range(9):
        parts = diffs if k % 2 else sums
        cos_out.append(wave_sum([(math.cos(unit * a * k), parts[a]) for a in range(len(parts))]))
        parts = odd_sums if k % 2 else odd_diffs
        sin_out.append(wave_sum([(math.sin(unit * a * k), parts[a]) for a in range(1, len(parts))]))
    return cos_out, sin_out


def split_value(value):
    high = value.astype(jnp.bfloat16)
    low = (value - high.astype(jnp.float32)).astype(jnp.bfloat16)
    return jnp.concatenate([high, low], axis=1)


def table_dot(high, low, pair):
    both = jnp.dot(high, pair, preferred_element_type=jnp.float32)
    rest = jnp.dot(low, pair[:, :LANES], preferred_element_type=jnp.float32)
    return both[:, :LANES] + both[:, LANES:] + rest


def kernel(
    bands,
    state_hbm, flag_ref, cut_ref, coef_hbm, fhi_hbm, flo_hbm, ihi_hbm, ilo_hbm, wave_hbm,
    out_hbm,
    state, result, winds, press, cuts, coef, fhi, flo, ihi, ilo, waves,
    halo_out, halo_in, send, recv, spectra, fields, bsend, brecv,
    load_sem, store_sem, halo_send, halo_recv, send_sem, recv_sem, bsend_sem, brecv_sem,
):
    lat = lax.axis_index("lat")
    lon = lax.axis_index("lon")
    rows, width = state_hbm.shape[0], state_hbm.shape[1]
    wide = recv.shape[1]
    spare = jnp.zeros((wide - width, LANES), jnp.float32)

    def field(row, part):
        return jnp.concatenate([state[row, :, pl.ds(part * LANES, LANES)], spare], axis=0)

    above = lax.rem(lat + bands - 1, bands)
    below = lax.rem(lat + 1, bands)
    chip = lon // 2
    core = lon % 2

    loads = [pltpu.make_async_copy(state_hbm, state, load_sem.at[0])]
    loads.append(pltpu.make_async_copy(coef_hbm.at[lat], coef, load_sem.at[1]))
    tables = ((fhi_hbm, fhi), (flo_hbm, flo), (ihi_hbm, ihi), (ilo_hbm, ilo), (wave_hbm, waves))
    for at, (source, target) in enumerate(tables):
        loads.append(pltpu.make_async_copy(source, target, load_sem.at[2 + at]))
    for load in loads:
        load.start()

    barrier = pltpu.get_barrier_semaphore()
    for offset in range(1, PARTS):
        pl.semaphore_signal(barrier, inc=1, device_id=(lat, lax.rem(lon + offset, PARTS)), device_id_type=MESH)
    pl.semaphore_signal(barrier, inc=1, device_id=(above, lon), device_id_type=MESH)
    pl.semaphore_signal(barrier, inc=1, device_id=(below, lon), device_id_type=MESH)

    lane = lax.broadcasted_iota(jnp.int32, (wide, LANES), 1)
    line = lax.broadcasted_iota(jnp.int32, (wide, LANES), 0)
    first = lane < 64
    block = (lane // 16) % 4
    for row in range(rows):
        kept = jnp.full((1, LANES), cut_ref[row], jnp.int32).astype(jnp.float32)
        flag = jnp.full((1, LANES), flag_ref[row], jnp.int32)
        cuts[pl.ds(row + 1, 1), :] = jnp.where(flag == 1, kept, OPEN_CUT)
    loads[0].wait()
    loads[1].wait()

    def prepare(row, carry):
        left = field(row, 0)
        right = field(row, 1)
        turned = pltpu.roll(right, 64, 1)
        step = jnp.where(lane < 63, pltpu.roll(turned, LANES - 1, 1), 0.0) - jnp.where(lane > 0, pltpu.roll(turned, 1, 1), 0.0)
        vert = right - 0.1 * step
        step = jnp.where(lane < 63, pltpu.roll(vert, LANES - 1, 1), 0.0) - jnp.where(lane > 0, pltpu.roll(vert, 1, 1), 0.0)
        press[row] = turned - 0.015 * step
        result[row, :, pl.ds(LANES, LANES)] = vert[:width]
        scale = coef[pl.ds(row, 1), :]
        zonal = left - scale * (pltpu.roll(turned, wide - 1, 0) - pltpu.roll(turned, 1, 0))
        north = field(jnp.minimum(row + 1, rows - 1), 1) * jnp.where(row < rows - 1, 0.015, 0.0)
        south = field(jnp.maximum(row - 1, 0), 1) * jnp.where(row > 0, 0.015, 0.0)
        winds[row + 1] = jnp.where(first, zonal, left - (north - south))
        return carry

    lax.fori_loop(0, rows, prepare, 0)
    for side, row in ((0, 0), (1, rows - 1)):
        turned = pltpu.roll(field(row, 1), 64, 1)
        message = jnp.where(first, turned, winds[row + 1])
        halo_out[side] = jnp.where(line == width, cuts[pl.ds(row + 1, 1), :], message)

    def pack(pair, slot):
        even = 2 * pair + 1
        sources = (
            jnp.where(first, winds[even], winds[even + 1]),
            jnp.where(first, winds[even + 1], winds[even]),
            jnp.where(first, press[even - 1], winds[even - 1]),
            jnp.where(first, press[even], winds[even + 2]),
        )
        for quarter in range(4):
            chunk = sources[quarter]
            for at in range(4):
                if at != quarter:
                    chunk = jnp.where(block == at, pltpu.roll(sources[at], (16 * (at - quarter)) % LANES, 1), chunk)
            send[slot + 2 * quarter] = chunk

    def pack_inner(at, carry):
        pack(1 + at, 8 * at)
        return carry

    def pack_outer(at, carry):
        pack(3 * at, 8 * at + 1)
        return carry

    lax.fori_loop(0, 2, pack_inner, 0)
    pl.semaphore_wait(barrier, PARTS + 1)

    halos = []
    for side, device in ((0, above), (1, below)):
        halos.append(
            pltpu.make_async_remote_copy(
                src_ref=halo_out.at[side],
                dst_ref=halo_in.at[1 - side],
                send_sem=halo_send.at[side],
                recv_sem=halo_recv.at[1 - side],
                device_id=(device, lon),
                device_id_type=MESH,
            )
        )
    for halo in halos:
        halo.start()

    def forward_copy(source, slot, device):
        return pltpu.make_async_remote_copy(
            src_ref=send.at[source],
            dst_ref=recv.at[slot],
            send_sem=send_sem.at[source],
            recv_sem=recv_sem.at[slot],
            device_id=(lat, device),
            device_id_type=MESH,
        )

    def backward_copy(source, slot, device):
        return pltpu.make_async_remote_copy(
            src_ref=bsend.at[source],
            dst_ref=brecv.at[slot],
            send_sem=bsend_sem.at[source],
            recv_sem=brecv_sem.at[slot],
            device_id=(lat, device),
            device_id_type=MESH,
        )

    order = (4, 3, 5, 2, 6, 1, 7, 0)

    def send_to(copy, kind):
        for offset in order:
            target = 2 * lax.rem(chip + offset, 8) + kind
            if offset:
                copy(target, lon, target).start()
            else:
                @pl.when(core != kind)
                def _():
                    copy(target, lon, target).start()

    send_to(forward_copy, 0)

    for side in range(2):
        halos[side].wait_recv()
    inside = jnp.where(lat > 0, 0.015, 0.0)
    upper = halo_in[0]
    cuts[pl.ds(0, 1), :] = upper[width : width + 1]
    winds[0] = jnp.where(line < width, upper - 0.015 * field(0, 1), 0.0)
    winds[1] = winds[1] + jnp.where(first | (line >= width), 0.0, inside * pltpu.roll(upper, 64, 1))
    inside = jnp.where(lat < bands - 1, 0.015, 0.0)
    lower = halo_in[1]
    cuts[pl.ds(rows + 1, 1), :] = lower[width : width + 1]
    winds[rows + 1] = jnp.where(line < width, lower + 0.015 * field(rows - 1, 1), 0.0)
    winds[rows] = winds[rows] - jnp.where(first | (line >= width), 0.0, inside * pltpu.roll(lower, 64, 1))

    lax.fori_loop(0, 2, pack_outer, 0)
    send_to(forward_copy, 1)
    recv[lon] = send[lon]

    half = chip // 4
    mine = (1 - core) * (1 + half) + core * 3 * half
    lanes = lax.broadcasted_iota(jnp.int32, (1, LANES), 1) // 16
    cut_even = cuts[pl.ds(2 * mine + 1, 1), :]
    cut_odd = cuts[pl.ds(2 * mine + 2, 1), :]
    limit = jnp.where((lanes == 0) | (lanes == 2) | (lanes == 5), cut_even, cut_odd)
    limit = jnp.where(lanes == 6, cuts[pl.ds(2 * mine, 1), :], limit)
    limit = jnp.where(lanes == 7, cuts[pl.ds(2 * mine + 3, 1), :], limit)
    factor = coef[pl.ds(8 + mine, 1), :]
    for load in loads[2:]:
        load.wait()

    def receive(offset, carry):
        source = lax.rem(lon + offset, PARTS)
        forward_copy(source, source, source).wait_recv()
        return carry

    lax.fori_loop(1, PARTS, receive, 0)

    def gather_waves(at, carry):
        where = pl.multiple_of(16 * at, 16)
        spans = pl.ds(where, 16)
        images = pl.ds(pl.multiple_of(wide + where, 16), 16)
        values = [recv[a, spans, :] for a in range(PARTS)]
        evens = [values[0]] + [values[a] + values[PARTS - a] for a in range(1, 8)] + [values[8]]
        odds = [None] + [values[a] - values[PARTS - a] for a in range(1, 8)]
        cos_out, sin_out = half_dft(evens, odds)
        spectra[0, spans, :] = split_value(cos_out[0])
        spectra[0, images, :] = split_value(cos_out[8])
        for k in range(1, 8):
            spectra[k, spans, :] = split_value(cos_out[k])
            spectra[k, images, :] = split_value(sin_out[k])
        return carry

    lax.fori_loop(0, wide // 16, gather_waves, 0)

    def transform(group, carry):
        values = table_dot(fhi[group], flo[group], spectra[group])
        wave = PARTS * line + group
        folded = jnp.where(line <= width // 2, PARTS * line, PARTS * (line - width // 2 - 1) + 8)
        wave = jnp.where(group > 0, jnp.minimum(wave, PARTS * width - wave), folded)
        ratio = limit / jnp.maximum(wave, 1).astype(jnp.float32)
        damping = jnp.minimum(1.0, ratio * ratio)
        real = values[:wide] * damping
        imag = values[wide:] * damping
        turn = factor * waves[group]
        zonal = lane < 32
        lift_real = jnp.where(zonal, turn * imag, factor * real)
        lift_imag = jnp.where(zonal, -turn * real, factor * imag)
        inner = (lane >= 32) & first
        outs = []
        for value, lift in ((real, lift_real), (imag, lift_imag)):
            total = pltpu.roll(lift, 32, 1) + pltpu.roll(lift, 96, 1) + pltpu.roll(lift, 64, 1)
            outs.append(jnp.where(inner, value + damping * total, value))
        both = split_value(jnp.concatenate(outs, axis=0))
        fields[group] = table_dot(ihi[group], ilo[group], both)
        return carry

    lax.fori_loop(0, 8, transform, 0)

    def scatter_waves(at, carry):
        where = pl.multiple_of(16 * at, 16)
        spans = pl.ds(where, 16)
        images = pl.ds(pl.multiple_of(wide + where, 16), 16)
        evens = [fields[0, spans, :]] + [fields[k, spans, :] for k in range(1, 8)] + [fields[0, images, :]]
        odds = [None] + [fields[k, images, :] for k in range(1, 8)]
        cos_out, sin_out = half_dft(evens, odds)
        circles[0, spans, :] = cos_out[0]
        circles[8, spans, :] = cos_out[8]
        for a in range(1, 8):
            circles[a, spans, :] = cos_out[a] - sin_out[a]
            circles[PARTS - a, spans, :] = cos_out[a] + sin_out[a]
        return carry

    circles = recv
    lax.fori_loop(0, wide // 16, scatter_waves, 0)
    narrow = lax.broadcasted_iota(jnp.int32, (24, LANES), 1)

    def pack_back(a, carry):
        rest = circles[a, pl.ds(72, 24), :]
        for at in range(3):
            spans = pl.ds(24 * at, 24)
            bsend[a, spans, :] = jnp.where(narrow < 96, circles[a, spans, :], pltpu.roll(rest, 96 - 32 * at, 1))
        return carry

    lax.fori_loop(0, PARTS, pack_back, 0)
    send_to(backward_copy, 0)
    send_to(backward_copy, 1)
    brecv[lon] = bsend[lon]

    def unpack(pair, slot):
        chunks = []
        for quarter in range(4):
            source = slot + 2 * quarter

            @pl.when(source != lon)
            def _():
                backward_copy(source, source, source).wait_recv()

            pieces = [brecv[source, pl.ds(24 * at, 24), :] for at in range(3)]
            rest = jnp.where(narrow < 32, pltpu.roll(pieces[0], 32, 1), pltpu.roll(pieces[1], 64, 1))
            rest = jnp.where(narrow < 64, rest, pltpu.roll(pieces[2], 96, 1))
            chunks.append(jnp.concatenate(pieces + [rest], axis=0))
        parts = []
        for at in range(4):
            shift = 64 if at >= 2 else 0
            part = None
            for quarter in range(4):
                amount = (16 * (quarter - at) + shift) % LANES
                moved = pltpu.roll(chunks[quarter], amount, 1) if amount else chunks[quarter]
                part = moved if part is None else jnp.where(block == quarter, moved, part)
            parts.append(part)
        even = 2 * pair
        spans = pl.ds(0, LANES)
        result[even, :, spans] = jnp.where(first, parts[0], parts[1])[:width]
        result[even + 1, :, spans] = jnp.where(first, parts[1], parts[0])[:width]
        spans = pl.ds(LANES, LANES)
        result[even, :, spans] = jnp.where(first[:width], result[even, :, spans], parts[2][:width])
        result[even + 1, :, spans] = jnp.where(first[:width], result[even + 1, :, spans], parts[3][:width])

    def store(pair):
        spans = pl.ds(2 * pair, 2)
        return pltpu.make_async_copy(result.at[spans], out_hbm.at[spans], store_sem.at[pair])

    def unpack_inner(at, carry):
        unpack(1 + at, 8 * at)
        store(1 + at).start()
        return carry

    def unpack_outer(at, carry):
        unpack(3 * at, 8 * at + 1)
        store(3 * at).start()
        return carry

    lax.fori_loop(0, 2, unpack_inner, 0)
    lax.fori_loop(0, 2, unpack_outer, 0)

    def finish(offset, carry):
        target = lax.rem(lon + offset, PARTS)
        forward_copy(target, lon, target).wait_send()
        backward_copy(target, lon, target).wait_send()
        return carry

    lax.fori_loop(1, PARTS, finish, 0)
    for halo in halos:
        halo.wait_send()
    for pair in range(rows // 2):
        store(pair).wait()


def solution(mesh):
    bands = mesh.shape["lat"]

    def body(state, filter_flag, cutoff):
        rows, width, depth = state.shape
        wide = (width + 2 + 15) // 16 * 16
        tables = dft_tables(width * PARTS, width, wide)
        coefs = coef_table(rows * bands, bands)
        f32 = jnp.float32
        table = pltpu.VMEM((8, 2 * wide, 2 * wide), jnp.bfloat16)
        any_spec = pl.BlockSpec(memory_space=pl.ANY)
        smem_spec = pl.BlockSpec(memory_space=pltpu.SMEM)
        dma = pltpu.SemaphoreType.DMA
        return pl.pallas_call(
            functools.partial(kernel, bands),
            out_shape=jax.ShapeDtypeStruct(state.shape, f32),
            in_specs=[any_spec, smem_spec, smem_spec] + [any_spec] * 6,
            out_specs=any_spec,
            scratch_shapes=[
                pltpu.VMEM(state.shape, f32),
                pltpu.VMEM(state.shape, f32),
                pltpu.VMEM((rows + 2, wide, LANES), f32),
                pltpu.VMEM((rows, wide, LANES), f32),
                pltpu.VMEM((16, LANES), f32),
                pltpu.VMEM((16, LANES), f32),
                table, table, table, table,
                pltpu.VMEM((8, wide, LANES), f32),
                pltpu.VMEM((2, wide, LANES), f32),
                pltpu.VMEM((2, wide, LANES), f32),
                pltpu.VMEM((PARTS, wide, LANES), f32),
                pltpu.VMEM((PARTS, wide, LANES), f32),
                pltpu.VMEM((8, 2 * wide, 2 * LANES), jnp.bfloat16),
                pltpu.VMEM((8, 2 * wide, LANES), f32),
                pltpu.VMEM((PARTS, PACKED, LANES), f32),
                pltpu.VMEM((PARTS, PACKED, LANES), f32),
                dma((7,)),
                dma((4,)),
                dma((2,)),
                dma((2,)),
                dma((PARTS,)),
                dma((PARTS,)),
                dma((PARTS,)),
                dma((PARTS,)),
            ],
            compiler_params=pltpu.CompilerParams(collective_id=0, has_side_effects=True),
        )(state, filter_flag, cutoff, coefs, *tables)

    return jax.shard_map(
        body,
        mesh=mesh,
        in_specs=(P("lat", "lon", None), P("lat"), P("lat")),
        out_specs=P("lat", "lon", None),
        check_vma=False,
    )
```

profile of v0, /device:TPU:1, one launch (start us, length us, event | category | flops | bytes accessed | tf_op | source)
XLA Modules:
  0.0 57.4 jit_solution(483562798655541091)
XLA Ops:
  0.0 2.2 %copy.10.state_hbm = f32[8,90,256]{2,1,0:T(8,128)} copy(f32[8,90,256]{2,0,1:T(8,128)} %param.9) | data formatting | bytes 1474560 | tf_op args[0]
  2.2 52.8 %shard_map.91 = f32[8,90,256]{2,1,0:T(8,128)} custom-call(f32[8,90,256]{2,1,0:T(8,128)} %copy.10.state_hbm, s32[8]{0:T(128)} %flag_ref.1, s32[8]{0:T(128)} %cut_ref.1, f32[32,16,128]{2,1,0:T(8,128)} %constant.12.clone.coef_hbm, bf16[8,192,192]{2,1,0:T(8,128)(2,1)} %constant.13.clone.fhi_hbm, bf16[8,192,192]{2,1,0:T(8,128)(2,1)} %constant.14.clone.flo_hbm, ...), custom_call_target="tpu_custom_call" | custom-call | tf_op jit(solution)/shard_map/pallas_call | solution.py:470
  55.0 2.4 %copy.11 = f32[8,90,256]{2,0,1:T(8,128)} copy(f32[8,90,256]{2,1,0:T(8,128)} %shard_map.91) | data formatting | bytes 1474560 | tf_op jit(solution)/shard_map/pallas_call | solution.py:470
where the time goes:
time: 57.7 us; the launch traced here: 57.4 us
  Pallas kernels  52.8 us (92%)
  local copies, waits for them, and re-layouts  4.66 us (8%)
    pallas_call x1, Pallas kernels, body(): pl.pallas_call(functools.partial(kernel, bands), out_shape=jax.ShapeDtype...  52.8 us
    pallas_call x1, local copies, waits for them, and re-layouts, body(): pl.pallas_call(functools.partial(kernel, bands), out_shape=jax.ShapeDtype...  2.43 us
    unnamed x1, local copies, waits for them, and re-layouts  2.23 us

commit v1 on v0

--- a/solution.py
+++ b/solution.py
@@ -68,8 +68,9 @@
                 inverse[0, part, row] = weight * cos_vals * inner
                 inverse[0, part, wide + row] = -weight * sin_vals * inner
             sines[group, row] = math.sin(2.0 * math.pi * wave / nlon)
-    waves = np.ascontiguousarray(np.broadcast_to(sines.astype(np.float32)[..., None], sines.shape + (LANES,)))
-    return split_table(forward) + split_table(inverse) + (waves,)
+    waves = np.zeros((wide, LANES), np.float32)
+    waves[:, :8] = sines.T
+    return np.concatenate(split_table(np.concatenate([forward, inverse])), axis=1), waves
 
 
 def coef_table(nlat, bands):
@@ -137,28 +138,28 @@
     return jnp.concatenate([high, low], axis=1)
 
 
-def table_dot(high, low, pair):
-    both = jnp.dot(high, pair, preferred_element_type=jnp.float32)
-    rest = jnp.dot(low, pair[:, :LANES], preferred_element_type=jnp.float32)
-    return both[:, :LANES] + both[:, LANES:] + rest
+def table_dot(table, pair):
+    both = jnp.dot(table, pair, preferred_element_type=jnp.float32)
+    half = table.shape[0] // 2
+    return both[:half, :LANES] + both[:half, LANES:] + both[half:, :LANES]
 
 
 def kernel(
     bands,
-    state_hbm, flag_ref, cut_ref, coef_hbm, fhi_hbm, flo_hbm, ihi_hbm, ilo_hbm, wave_hbm,
+    state_hbm, flag_ref, cut_ref, coef_hbm, table_hbm, wave_hbm,
     out_hbm,
-    state, result, winds, press, cuts, coef, fhi, flo, ihi, ilo, waves,
+    state, result, winds, press, cuts, coef, table, waves, damps, turns,
     halo_out, halo_in, send, recv, spectra, fields, bsend, brecv,
     load_sem, store_sem, halo_send, halo_recv, send_sem, recv_sem, bsend_sem, brecv_sem,
 ):
     lat = lax.axis_index("lat")
     lon = lax.axis_index("lon")
-    rows, width = state_hbm.shape[0], state_hbm.shape[1]
+    width, rows = state_hbm.shape[0], state_hbm.shape[1]
     wide = recv.shape[1]
     spare = jnp.zeros((wide - width, LANES), jnp.float32)
 
     def field(row, part):
-        return jnp.concatenate([state[row, :, pl.ds(part * LANES, LANES)], spare], axis=0)
+        return jnp.concatenate([state[:, row, pl.ds(part * LANES, LANES)], spare], axis=0)
 
     above = lax.rem(lat + bands - 1, bands)
     below = lax.rem(lat + 1, bands)
@@ -167,11 +168,11 @@
 
     loads = [pltpu.make_async_copy(state_hbm, state, load_sem.at[0])]
     loads.append(pltpu.make_async_copy(coef_hbm.at[lat], coef, load_sem.at[1]))
-    tables = ((fhi_hbm, fhi), (flo_hbm, flo), (ihi_hbm, ihi), (ilo_hbm, ilo), (wave_hbm, waves))
+    tables = ((wave_hbm, waves), (table_hbm, table))
     for at, (source, target) in enumerate(tables):
         loads.append(pltpu.make_async_copy(source, target, load_sem.at[2 + at]))
-    for load in loads:
-        load.start()
+    loads[0].start()
+    loads[1].start()
 
     barrier = pltpu.get_barrier_semaphore()
     for offset in range(1, PARTS):
@@ -189,8 +190,10 @@
         cuts[pl.ds(row + 1, 1), :] = jnp.where(flag == 1, kept, OPEN_CUT)
     loads[0].wait()
     loads[1].wait()
-
-    def prepare(row, carry):
+    for load in loads[2:]:
+        load.start()
+
+    def prepare(row):
         left = field(row, 0)
         right = field(row, 1)
         turned = pltpu.roll(right, 64, 1)
@@ -198,15 +201,18 @@
         vert = right - 0.1 * step
         step = jnp.where(lane < 63, pltpu.roll(vert, LANES - 1, 1), 0.0) - jnp.where(lane > 0, pltpu.roll(vert, 1, 1), 0.0)
         press[row] = turned - 0.015 * step
-        result[row, :, pl.ds(LANES, LANES)] = vert[:width]
+        result[:, row, pl.ds(LANES, LANES)] = vert[:width]
         scale = coef[pl.ds(row, 1), :]
         zonal = left - scale * (pltpu.roll(turned, wide - 1, 0) - pltpu.roll(turned, 1, 0))
-        north = field(jnp.minimum(row + 1, rows - 1), 1) * jnp.where(row < rows - 1, 0.015, 0.0)
-        south = field(jnp.maximum(row - 1, 0), 1) * jnp.where(row > 0, 0.015, 0.0)
-        winds[row + 1] = jnp.where(first, zonal, left - (north - south))
-        return carry
-
-    lax.fori_loop(0, rows, prepare, 0)
+        merid = left
+        if row < rows - 1:
+            merid = merid - 0.015 * field(row + 1, 1)
+        if row > 0:
+            merid = merid + 0.015 * field(row - 1, 1)
+        winds[row + 1] = jnp.where(first, zonal, merid)
+
+    for row in range(rows):
+        prepare(row)
     for side, row in ((0, 0), (1, rows - 1)):
         turned = pltpu.roll(field(row, 1), 64, 1)
         message = jnp.where(first, turned, winds[row + 1])
@@ -235,7 +241,7 @@
         pack(3 * at, 8 * at + 1)
         return carry
 
-    lax.fori_loop(0, 2, pack_inner, 0)
+    lax.fori_loop(0, 2, pack_inner, 0, unroll=2)
     pl.semaphore_wait(barrier, PARTS + 1)
 
     halos = []
@@ -300,7 +306,7 @@
     winds[rows + 1] = jnp.where(line < width, lower + 0.015 * field(rows - 1, 1), 0.0)
     winds[rows] = winds[rows] - jnp.where(first | (line >= width), 0.0, inside * pltpu.roll(lower, 64, 1))
 
-    lax.fori_loop(0, 2, pack_outer, 0)
+    lax.fori_loop(0, 2, pack_outer, 0, unroll=2)
     send_to(forward_copy, 1)
     recv[lon] = send[lon]
 
@@ -313,7 +319,18 @@
     limit = jnp.where(lanes == 6, cuts[pl.ds(2 * mine, 1), :], limit)
     limit = jnp.where(lanes == 7, cuts[pl.ds(2 * mine + 3, 1), :], limit)
     factor = coef[pl.ds(8 + mine, 1), :]
-    for load in loads[2:]:
+    loads[2].wait()
+
+    for group in range(8):
+        wave = PARTS * line + group
+        if group:
+            wave = jnp.minimum(wave, PARTS * width - wave)
+        else:
+            wave = jnp.where(line <= width // 2, wave, PARTS * (line - width // 2 - 1) + 8)
+        ratio = limit / jnp.maximum(wave, 1).astype(jnp.float32)
+        damps[group] = jnp.minimum(1.0, ratio * ratio)
+        turns[group] = factor * waves[:, group : group + 1]
+    for load in loads[3:]:
         load.wait()
 
     def receive(offset, carry):
@@ -338,18 +355,14 @@
             spectra[k, images, :] = split_value(sin_out[k])
         return carry
 
-    lax.fori_loop(0, wide // 16, gather_waves, 0)
+    lax.fori_loop(0, wide // 16, gather_waves, 0, unroll=6)
 
     def transform(group, carry):
-        values = table_dot(fhi[group], flo[group], spectra[group])
-        wave = PARTS * line + group
-        folded = jnp.where(line <= width // 2, PARTS * line, PARTS * (line - width // 2 - 1) + 8)
-        wave = jnp.where(group > 0, jnp.minimum(wave, PARTS * width - wave), folded)
-        ratio = limit / jnp.maximum(wave, 1).astype(jnp.float32)
-        damping = jnp.minimum(1.0, ratio * ratio)
+        values = table_dot(table[group], spectra[group])
+        damping = damps[group]
         real = values[:wide] * damping
         imag = values[wide:] * damping
-        turn = factor * waves[group]
+        turn = turns[group]
         zonal = lane < 32
         lift_real = jnp.where(zonal, turn * imag, factor * real)
         lift_imag = jnp.where(zonal, -turn * real, factor * imag)
@@ -359,10 +372,10 @@
             total = pltpu.roll(lift, 32, 1) + pltpu.roll(lift, 96, 1) + pltpu.roll(lift, 64, 1)
             outs.append(jnp.where(inner, value + damping * total, value))
         both = split_value(jnp.concatenate(outs, axis=0))
-        fields[group] = table_dot(ihi[group], ilo[group], both)
-        return carry
-
-    lax.fori_loop(0, 8, transform, 0)
+        fields[group] = table_dot(table[8 + group], both)
+        return carry
+
+    lax.fori_loop(0, 8, transform, 0, unroll=8)
 
     def scatter_waves(at, carry):
         where = pl.multiple_of(16 * at, 16)
@@ -379,7 +392,7 @@
         return carry
 
     circles = recv
-    lax.fori_loop(0, wide // 16, scatter_waves, 0)
+    lax.fori_loop(0, wide // 16, scatter_waves, 0, unroll=6)
     narrow = lax.broadcasted_iota(jnp.int32, (24, LANES), 1)
 
     def pack_back(a, carry):
@@ -389,7 +402,7 @@
             bsend[a, spans, :] = jnp.where(narrow < 96, circles[a, spans, :], pltpu.roll(rest, 96 - 32 * at, 1))
         return carry
 
-    lax.fori_loop(0, PARTS, pack_back, 0)
+    lax.fori_loop(0, PARTS, pack_back, 0, unroll=PARTS)
     send_to(backward_copy, 0)
     send_to(backward_copy, 1)
     brecv[lon] = bsend[lon]
@@ -418,28 +431,18 @@
             parts.append(part)
         even = 2 * pair
         spans = pl.ds(0, LANES)
-        result[even, :, spans] = jnp.where(first, parts[0], parts[1])[:width]
-        result[even + 1, :, spans] = jnp.where(first, parts[1], parts[0])[:width]
+        result[:, even, spans] = jnp.where(first, parts[0], parts[1])[:width]
+        result[:, even + 1, spans] = jnp.where(first, parts[1], parts[0])[:width]
         spans = pl.ds(LANES, LANES)
-        result[even, :, spans] = jnp.where(first[:width], result[even, :, spans], parts[2][:width])
-        result[even + 1, :, spans] = jnp.where(first[:width], result[even + 1, :, spans], parts[3][:width])
-
-    def store(pair):
-        spans = pl.ds(2 * pair, 2)
-        return pltpu.make_async_copy(result.at[spans], out_hbm.at[spans], store_sem.at[pair])
-
-    def unpack_inner(at, carry):
+        result[:, even, spans] = jnp.where(first[:width], result[:, even, spans], parts[2][:width])
+        result[:, even + 1, spans] = jnp.where(first[:width], result[:, even + 1, spans], parts[3][:width])
+
+    for at in range(2):
         unpack(1 + at, 8 * at)
-        store(1 + at).start()
-        return carry
-
-    def unpack_outer(at, carry):
+    for at in range(2):
         unpack(3 * at, 8 * at + 1)
-        store(3 * at).start()
-        return carry
-
-    lax.fori_loop(0, 2, unpack_inner, 0)
-    lax.fori_loop(0, 2, unpack_outer, 0)
+    store = pltpu.make_async_copy(result, out_hbm, store_sem.at[0])
+    store.start()
 
     def finish(offset, carry):
         target = lax.rem(lon + offset, PARTS)
@@ -450,8 +453,7 @@
     lax.fori_loop(1, PARTS, finish, 0)
     for halo in halos:
         halo.wait_send()
-    for pair in range(rows // 2):
-        store(pair).wait()
+    store.wait()
 
 
 def solution(mesh):
@@ -463,23 +465,26 @@
         tables = dft_tables(width * PARTS, width, wide)
         coefs = coef_table(rows * bands, bands)
         f32 = jnp.float32
-        table = pltpu.VMEM((8, 2 * wide, 2 * wide), jnp.bfloat16)
+        table = pltpu.VMEM((16, 4 * wide, 2 * wide), jnp.bfloat16)
         any_spec = pl.BlockSpec(memory_space=pl.ANY)
+        hbm_spec = pl.BlockSpec(memory_space=pltpu.HBM)
         smem_spec = pl.BlockSpec(memory_space=pltpu.SMEM)
         dma = pltpu.SemaphoreType.DMA
-        return pl.pallas_call(
+        result = pl.pallas_call(
             functools.partial(kernel, bands),
-            out_shape=jax.ShapeDtypeStruct(state.shape, f32),
-            in_specs=[any_spec, smem_spec, smem_spec] + [any_spec] * 6,
+            out_shape=jax.ShapeDtypeStruct((width, rows, depth), f32),
+            in_specs=[hbm_spec, smem_spec, smem_spec] + [hbm_spec] * 3,
             out_specs=any_spec,
             scratch_shapes=[
-                pltpu.VMEM(state.shape, f32),
-                pltpu.VMEM(state.shape, f32),
+                pltpu.VMEM((width, rows, depth), f32),
+                pltpu.VMEM((width, rows, depth), f32),
                 pltpu.VMEM((rows + 2, wide, LANES), f32),
                 pltpu.VMEM((rows, wide, LANES), f32),
                 pltpu.VMEM((16, LANES), f32),
                 pltpu.VMEM((16, LANES), f32),
-                table, table, table, table,
+                table,
+                pltpu.VMEM((wide, LANES), f32),
+                pltpu.VMEM((8, wide, LANES), f32),
                 pltpu.VMEM((8, wide, LANES), f32),
                 pltpu.VMEM((2, wide, LANES), f32),
                 pltpu.VMEM((2, wide, LANES), f32),
@@ -489,8 +494,8 @@
                 pltpu.VMEM((8, 2 * wide, LANES), f32),
                 pltpu.VMEM((PARTS, PACKED, LANES), f32),
                 pltpu.VMEM((PARTS, PACKED, LANES), f32),
-                dma((7,)),
                 dma((4,)),
+                dma((1,)),
                 dma((2,)),
                 dma((2,)),
                 dma((PARTS,)),
@@ -498,8 +503,9 @@
                 dma((PARTS,)),
                 dma((PARTS,)),
             ],
-            compiler_params=pltpu.CompilerParams(collective_id=0, has_side_effects=True),
-        )(state, filter_flag, cutoff, coefs, *tables)
+            compiler_params=pltpu.CompilerParams(collective_id=0, has_side_effects=True, vmem_limit_bytes=60 << 20),
+        )(jnp.transpose(state, (1, 0, 2)), filter_flag, cutoff, coefs, *tables)
+        return jnp.transpose(result, (1, 0, 2))
 
     return jax.shard_map(
         body,

time: 57.7 us -> 51.6 us (0.89)
  Pallas kernels: 52.8 us -> 49.4 us
  local copies, waits for them, and re-layouts: 4.66 us -> 2.03 us
    pallas_call x1, Pallas kernels: 52.8 us -> 49.4 us  [body(): pl.pallas_call(functools.partial(kernel, bands), out_shape=jax.ShapeDtype...]
    pallas_call x1 -> x0, local copies, waits for them, and re-layouts: 2.43 us -> none  [body(): pl.pallas_call(functools.partial(kernel, bands), out_shape=jax.ShapeDtype...]
where the time goes in v1:
time: 51.6 us; the launch traced here: 51.4 us
  Pallas kernels  49.4 us (96%)
  local copies, waits for them, and re-layouts  2.03 us (4%)
    pallas_call x1, Pallas kernels, body(): pl.pallas_call(functools.partial(kernel, bands), out_shape=jax.ShapeDtype...  49.4 us
    unnamed x1, local copies, waits for them, and re-layouts  2.03 us

profile of v1, /device:TPU:1, one launch (start us, length us, event | category | flops | bytes accessed | tf_op | source)
XLA Modules:
  0.0 51.4 jit_solution(13386172585934586093)
XLA Ops:
  0.0 49.4 %shard_map.64 = f32[90,8,256]{2,1,0:T(8,128)} custom-call(f32[90,8,256]{2,1,0:T(8,128)} %bitcast.3, s32[8]{0:T(128)} %flag_ref.1, s32[8]{0:T(128)} %cut_ref.1, f32[32,16,128]{2,1,0:T(8,128)} %constant.6.clone.coef_hbm, bf16[16,384,192]{2,1,0:T(8,128)(2,1)} %constant.7.clone.table_hbm, f32[96,128]{1,0:T(8,128)} %constant.8.clone.wave_hbm), custom_call_target="tpu_custom_call" | custom-call | tf_op jit(solution)/shard_map/pallas_call | solution.py:473
  49.4 2.0 %copy.8 = f32[8,90,256]{2,0,1:T(8,128)} copy(f32[8,90,256]{2,0,1:T(8,128)} %bitcast.2) | data formatting | bytes 1474560

commit v2 on v1

--- a/solution.py
+++ b/solution.py
@@ -146,9 +146,9 @@
 
 def kernel(
     bands,
-    state_hbm, flag_ref, cut_ref, coef_hbm, table_hbm, wave_hbm,
+    state_hbm, flag_hbm, cut_hbm, coef_hbm, table_hbm, wave_hbm,
     out_hbm,
-    state, result, winds, press, cuts, coef, table, waves, damps, turns,
+    state, flag_ref, cut_ref, result, winds, press, cuts, coef, table, waves, damps, turns,
     halo_out, halo_in, send, recv, spectra, fields, bsend, brecv,
     load_sem, store_sem, halo_send, halo_recv, send_sem, recv_sem, bsend_sem, brecv_sem,
 ):
@@ -168,11 +168,13 @@
 
     loads = [pltpu.make_async_copy(state_hbm, state, load_sem.at[0])]
     loads.append(pltpu.make_async_copy(coef_hbm.at[lat], coef, load_sem.at[1]))
+    loads.append(pltpu.make_async_copy(flag_hbm, flag_ref, load_sem.at[2]))
+    loads.append(pltpu.make_async_copy(cut_hbm, cut_ref, load_sem.at[3]))
     tables = ((wave_hbm, waves), (table_hbm, table))
     for at, (source, target) in enumerate(tables):
-        loads.append(pltpu.make_async_copy(source, target, load_sem.at[2 + at]))
-    loads[0].start()
-    loads[1].start()
+        loads.append(pltpu.make_async_copy(source, target, load_sem.at[4 + at]))
+    for load in loads[:4]:
+        load.start()
 
     barrier = pltpu.get_barrier_semaphore()
     for offset in range(1, PARTS):
@@ -184,14 +186,14 @@
     line = lax.broadcasted_iota(jnp.int32, (wide, LANES), 0)
     first = lane < 64
     block = (lane // 16) % 4
+    for load in loads[:4]:
+        load.wait()
+    for load in loads[4:]:
+        load.start()
     for row in range(rows):
         kept = jnp.full((1, LANES), cut_ref[row], jnp.int32).astype(jnp.float32)
         flag = jnp.full((1, LANES), flag_ref[row], jnp.int32)
         cuts[pl.ds(row + 1, 1), :] = jnp.where(flag == 1, kept, OPEN_CUT)
-    loads[0].wait()
-    loads[1].wait()
-    for load in loads[2:]:
-        load.start()
 
     def prepare(row):
         left = field(row, 0)
@@ -319,7 +321,7 @@
     limit = jnp.where(lanes == 6, cuts[pl.ds(2 * mine, 1), :], limit)
     limit = jnp.where(lanes == 7, cuts[pl.ds(2 * mine + 3, 1), :], limit)
     factor = coef[pl.ds(8 + mine, 1), :]
-    loads[2].wait()
+    loads[4].wait()
 
     for group in range(8):
         wave = PARTS * line + group
@@ -330,7 +332,7 @@
         ratio = limit / jnp.maximum(wave, 1).astype(jnp.float32)
         damps[group] = jnp.minimum(1.0, ratio * ratio)
         turns[group] = factor * waves[:, group : group + 1]
-    for load in loads[3:]:
+    for load in loads[5:]:
         load.wait()
 
     def receive(offset, carry):
@@ -468,15 +470,17 @@
         table = pltpu.VMEM((16, 4 * wide, 2 * wide), jnp.bfloat16)
         any_spec = pl.BlockSpec(memory_space=pl.ANY)
         hbm_spec = pl.BlockSpec(memory_space=pltpu.HBM)
-        smem_spec = pl.BlockSpec(memory_space=pltpu.SMEM)
         dma = pltpu.SemaphoreType.DMA
+        operands = (jnp.transpose(state, (1, 0, 2)), filter_flag, cutoff) + tuple(map(jnp.asarray, (coefs,) + tables))
         result = pl.pallas_call(
             functools.partial(kernel, bands),
             out_shape=jax.ShapeDtypeStruct((width, rows, depth), f32),
-            in_specs=[hbm_spec, smem_spec, smem_spec] + [hbm_spec] * 3,
+            in_specs=[hbm_spec] * 6,
             out_specs=any_spec,
             scratch_shapes=[
                 pltpu.VMEM((width, rows, depth), f32),
+                pltpu.SMEM((rows,), jnp.int32),
+                pltpu.SMEM((rows,), jnp.int32),
                 pltpu.VMEM((width, rows, depth), f32),
                 pltpu.VMEM((rows + 2, wide, LANES), f32),
                 pltpu.VMEM((rows, wide, LANES), f32),
@@ -494,7 +498,7 @@
                 pltpu.VMEM((8, 2 * wide, LANES), f32),
                 pltpu.VMEM((PARTS, PACKED, LANES), f32),
                 pltpu.VMEM((PARTS, PACKED, LANES), f32),
-                dma((4,)),
+                dma((6,)),
                 dma((1,)),
                 dma((2,)),
                 dma((2,)),
@@ -503,8 +507,8 @@
                 dma((PARTS,)),
                 dma((PARTS,)),
             ],
-            compiler_params=pltpu.CompilerParams(collective_id=0, has_side_effects=True, vmem_limit_bytes=60 << 20),
-        )(jnp.transpose(state, (1, 0, 2)), filter_flag, cutoff, coefs, *tables)
+            compiler_params=pltpu.CompilerParams(collective_id=0, has_side_effects=True, vmem_limit_bytes=32 << 20),
+        )(*(pltpu.with_memory_space_constraint(value, pltpu.HBM) for value in operands))
         return jnp.transpose(result, (1, 0, 2))
 
     return jax.shard_map(

time: 51.6 us -> 49.4 us (0.957)
  local copies, waits for them, and re-layouts: 2.03 us -> 0.87 us
  Pallas kernels: 49.4 us -> 48.4 us
    unnamed x1, local copies, waits for them, and re-layouts: 2.03 us -> 0.87 us
    pallas_call x1, Pallas kernels: 49.4 us -> 48.4 us  [body(): pl.pallas_call(functools.partial(kernel, bands), out_shape=jax.ShapeDtype...]
where the time goes in v2:
time: 49.4 us; the launch traced here: 49.3 us
  Pallas kernels  48.4 us (98%)
  local copies, waits for them, and re-layouts  0.87 us (2%)
    pallas_call x1, Pallas kernels, body(): pl.pallas_call(functools.partial(kernel, bands), out_shape=jax.ShapeDtype...  48.4 us

profile of v2, /device:TPU:1, one launch (start us, length us, event | category | flops | bytes accessed | tf_op | source)
XLA Modules:
  0.0 49.3 jit_solution(18008293205046048757)
XLA Ops:
  0.0 48.4 %shard_map.64 = f32[90,8,256]{2,1,0:T(8,128)S(1)} custom-call(f32[90,8,256]{2,1,0:T(8,128)} %bitcast.3, s32[8]{0:T(128)} %flag_hbm.1, s32[8]{0:T(128)} %cut_hbm.1, f32[32,16,128]{2,1,0:T(8,128)} %constant.6.clone.coef_hbm, bf16[16,384,192]{2,1,0:T(8,128)(2,1)} %constant.7.clone.table_hbm, f32[96,128]{1,0:T(8,128)} %constant.8.clone.wave_hbm), custom_call_target="tpu_custom_call" | custom-call | tf_op jit(solution)/shard_map/pallas_call | solution.py:475
  48.4 0.9 %copy.8 = f32[8,90,256]{2,0,1:T(8,128)} copy(f32[8,90,256]{2,0,1:T(8,128)S(1)} %bitcast.2) | data formatting | bytes 1474560

commit v3 on v2

--- a/solution.py
+++ b/solution.py
@@ -147,10 +147,10 @@
 def kernel(
     bands,
     state_hbm, flag_hbm, cut_hbm, coef_hbm, table_hbm, wave_hbm,
-    out_hbm,
-    state, flag_ref, cut_ref, result, winds, press, cuts, coef, table, waves, damps, turns,
+    result,
+    state, flag_ref, cut_ref, winds, press, slopes, cuts, coef, table, waves, damps, turns,
     halo_out, halo_in, send, recv, spectra, fields, bsend, brecv,
-    load_sem, store_sem, halo_send, halo_recv, send_sem, recv_sem, bsend_sem, brecv_sem,
+    load_sem, halo_send, halo_recv, send_sem, recv_sem, bsend_sem, brecv_sem,
 ):
     lat = lax.axis_index("lat")
     lon = lax.axis_index("lon")
@@ -166,14 +166,18 @@
     chip = lon // 2
     core = lon % 2
 
-    loads = [pltpu.make_async_copy(state_hbm, state, load_sem.at[0])]
-    loads.append(pltpu.make_async_copy(coef_hbm.at[lat], coef, load_sem.at[1]))
-    loads.append(pltpu.make_async_copy(flag_hbm, flag_ref, load_sem.at[2]))
-    loads.append(pltpu.make_async_copy(cut_hbm, cut_ref, load_sem.at[3]))
+    def state_copy(part):
+        spans = pl.ds(part * LANES, LANES)
+        return pltpu.make_async_copy(state_hbm.at[:, :, spans], state.at[:, :, spans], load_sem.at[part])
+
+    loads = [state_copy(1), state_copy(0)]
+    loads.append(pltpu.make_async_copy(coef_hbm.at[lat], coef, load_sem.at[2]))
+    loads.append(pltpu.make_async_copy(flag_hbm, flag_ref, load_sem.at[3]))
+    loads.append(pltpu.make_async_copy(cut_hbm, cut_ref, load_sem.at[4]))
     tables = ((wave_hbm, waves), (table_hbm, table))
     for at, (source, target) in enumerate(tables):
-        loads.append(pltpu.make_async_copy(source, target, load_sem.at[4 + at]))
-    for load in loads[:4]:
+        loads.append(pltpu.make_async_copy(source, target, load_sem.at[5 + at]))
+    for load in loads[:5]:
         load.start()
 
     barrier = pltpu.get_barrier_semaphore()
@@ -186,17 +190,8 @@
     line = lax.broadcasted_iota(jnp.int32, (wide, LANES), 0)
     first = lane < 64
     block = (lane // 16) % 4
-    for load in loads[:4]:
-        load.wait()
-    for load in loads[4:]:
-        load.start()
+    loads[0].wait()
     for row in range(rows):
-        kept = jnp.full((1, LANES), cut_ref[row], jnp.int32).astype(jnp.float32)
-        flag = jnp.full((1, LANES), flag_ref[row], jnp.int32)
-        cuts[pl.ds(row + 1, 1), :] = jnp.where(flag == 1, kept, OPEN_CUT)
-
-    def prepare(row):
-        left = field(row, 0)
         right = field(row, 1)
         turned = pltpu.roll(right, 64, 1)
         step = jnp.where(lane < 63, pltpu.roll(turned, LANES - 1, 1), 0.0) - jnp.where(lane > 0, pltpu.roll(turned, 1, 1), 0.0)
@@ -204,21 +199,19 @@
         step = jnp.where(lane < 63, pltpu.roll(vert, LANES - 1, 1), 0.0) - jnp.where(lane > 0, pltpu.roll(vert, 1, 1), 0.0)
         press[row] = turned - 0.015 * step
         result[:, row, pl.ds(LANES, LANES)] = vert[:width]
-        scale = coef[pl.ds(row, 1), :]
-        zonal = left - scale * (pltpu.roll(turned, wide - 1, 0) - pltpu.roll(turned, 1, 0))
+        slopes[row] = pltpu.roll(turned, wide - 1, 0) - pltpu.roll(turned, 1, 0)
+    for load in loads[1:3]:
+        load.wait()
+
+    def prepare(row):
+        left = field(row, 0)
+        zonal = left - coef[pl.ds(row, 1), :] * slopes[row]
         merid = left
         if row < rows - 1:
             merid = merid - 0.015 * field(row + 1, 1)
         if row > 0:
             merid = merid + 0.015 * field(row - 1, 1)
         winds[row + 1] = jnp.where(first, zonal, merid)
-
-    for row in range(rows):
-        prepare(row)
-    for side, row in ((0, 0), (1, rows - 1)):
-        turned = pltpu.roll(field(row, 1), 64, 1)
-        message = jnp.where(first, turned, winds[row + 1])
-        halo_out[side] = jnp.where(line == width, cuts[pl.ds(row + 1, 1), :], message)
 
     def pack(pair, slot):
         even = 2 * pair + 1
@@ -235,17 +228,6 @@
                     chunk = jnp.where(block == at, pltpu.roll(sources[at], (16 * (at - quarter)) % LANES, 1), chunk)
             send[slot + 2 * quarter] = chunk
 
-    def pack_inner(at, carry):
-        pack(1 + at, 8 * at)
-        return carry
-
-    def pack_outer(at, carry):
-        pack(3 * at, 8 * at + 1)
-        return carry
-
-    lax.fori_loop(0, 2, pack_inner, 0, unroll=2)
-    pl.semaphore_wait(barrier, PARTS + 1)
-
     halos = []
     for side, device in ((0, above), (1, below)):
         halos.append(
@@ -258,9 +240,6 @@
                 device_id_type=MESH,
             )
         )
-    for halo in halos:
-        halo.start()
-
     def forward_copy(source, slot, device):
         return pltpu.make_async_remote_copy(
             src_ref=send.at[source],
@@ -293,7 +272,39 @@
                 def _():
                     copy(target, lon, target).start()
 
-    send_to(forward_copy, 0)
+    def pack_and_send(pair, at, kind):
+        pack(pair, 8 * at + kind)
+        if pair == 1:
+            pl.semaphore_wait(barrier, PARTS + 1)
+        for offset in range(4):
+            target = 8 * at + 2 * lax.rem(chip + offset, 4) + kind
+
+            @pl.when(target != lon)
+            def _():
+                forward_copy(target, lon, target).start()
+
+    for row in range(1, 5):
+        prepare(row)
+    pack_and_send(1, 0, 0)
+    for row in range(5, 7):
+        prepare(row)
+    pack_and_send(2, 1, 0)
+    prepare(0)
+    prepare(rows - 1)
+    for load in loads[3:5]:
+        load.wait()
+    for load in loads[5:]:
+        load.start()
+    for row in range(rows):
+        kept = jnp.full((1, LANES), cut_ref[row], jnp.int32).astype(jnp.float32)
+        flag = jnp.full((1, LANES), flag_ref[row], jnp.int32)
+        cuts[pl.ds(row + 1, 1), :] = jnp.where(flag == 1, kept, OPEN_CUT)
+    for side, row in ((0, 0), (1, rows - 1)):
+        turned = pltpu.roll(field(row, 1), 64, 1)
+        message = jnp.where(first, turned, winds[row + 1])
+        halo_out[side] = jnp.where(line == width, cuts[pl.ds(row + 1, 1), :], message)
+    for halo in halos:
+        halo.start()
 
     for side in range(2):
         halos[side].wait_recv()
@@ -308,8 +319,8 @@
     winds[rows + 1] = jnp.where(line < width, lower + 0.015 * field(rows - 1, 1), 0.0)
     winds[rows] = winds[rows] - jnp.where(first | (line >= width), 0.0, inside * pltpu.roll(lower, 64, 1))
 
-    lax.fori_loop(0, 2, pack_outer, 0, unroll=2)
-    send_to(forward_copy, 1)
+    pack_and_send(0, 0, 1)
+    pack_and_send(3, 1, 1)
     recv[lon] = send[lon]
 
     half = chip // 4
@@ -321,7 +332,7 @@
     limit = jnp.where(lanes == 6, cuts[pl.ds(2 * mine, 1), :], limit)
     limit = jnp.where(lanes == 7, cuts[pl.ds(2 * mine + 3, 1), :], limit)
     factor = coef[pl.ds(8 + mine, 1), :]
-    loads[4].wait()
+    loads[5].wait()
 
     for group in range(8):
         wave = PARTS * line + group
@@ -332,7 +343,7 @@
         ratio = limit / jnp.maximum(wave, 1).astype(jnp.float32)
         damps[group] = jnp.minimum(1.0, ratio * ratio)
         turns[group] = factor * waves[:, group : group + 1]
-    for load in loads[5:]:
+    for load in loads[6:]:
         load.wait()
 
     def receive(offset, carry):
@@ -443,8 +454,6 @@
         unpack(1 + at, 8 * at)
     for at in range(2):
         unpack(3 * at, 8 * at + 1)
-    store = pltpu.make_async_copy(result, out_hbm, store_sem.at[0])
-    store.start()
 
     def finish(offset, carry):
         target = lax.rem(lon + offset, PARTS)
@@ -455,7 +464,6 @@
     lax.fori_loop(1, PARTS, finish, 0)
     for halo in halos:
         halo.wait_send()
-    store.wait()
 
 
 def solution(mesh):
@@ -468,7 +476,6 @@
         coefs = coef_table(rows * bands, bands)
         f32 = jnp.float32
         table = pltpu.VMEM((16, 4 * wide, 2 * wide), jnp.bfloat16)
-        any_spec = pl.BlockSpec(memory_space=pl.ANY)
         hbm_spec = pl.BlockSpec(memory_space=pltpu.HBM)
         dma = pltpu.SemaphoreType.DMA
         operands = (jnp.transpose(state, (1, 0, 2)), filter_flag, cutoff) + tuple(map(jnp.asarray, (coefs,) + tables))
@@ -476,13 +483,13 @@
             functools.partial(kernel, bands),
             out_shape=jax.ShapeDtypeStruct((width, rows, depth), f32),
             in_specs=[hbm_spec] * 6,
-            out_specs=any_spec,
+            out_specs=pl.BlockSpec(memory_space=pltpu.VMEM),
             scratch_shapes=[
                 pltpu.VMEM((width, rows, depth), f32),
                 pltpu.SMEM((rows,), jnp.int32),
                 pltpu.SMEM((rows,), jnp.int32),
-                pltpu.VMEM((width, rows, depth), f32),
                 pltpu.VMEM((rows + 2, wide, LANES), f32),
+                pltpu.VMEM((rows, wide, LANES), f32),
                 pltpu.VMEM((rows, wide, LANES), f32),
                 pltpu.VMEM((16, LANES), f32),
                 pltpu.VMEM((16, LANES), f32),
@@ -498,8 +505,7 @@
                 pltpu.VMEM((8, 2 * wide, LANES), f32),
                 pltpu.VMEM((PARTS, PACKED, LANES), f32),
                 pltpu.VMEM((PARTS, PACKED, LANES), f32),
-                dma((6,)),
-                dma((1,)),
+                dma((7,)),
                 dma((2,)),
                 dma((2,)),
                 dma((PARTS,)),

time: 49.4 us -> 48.9 us (0.990)
  Pallas kernels: 48.4 us -> 47.9 us
    pallas_call x1, Pallas kernels: 48.4 us -> 47.9 us  [body(): pl.pallas_call(functools.partial(kernel, bands), out_shape=jax.ShapeDtype...]
where the time goes in v3:
time: 48.9 us; the launch traced here: 48.8 us
  Pallas kernels  47.9 us (98%)
  local copies, waits for them, and re-layouts  0.87 us (2%)
    pallas_call x1, Pallas kernels, body(): pl.pallas_call(functools.partial(kernel, bands), out_shape=jax.ShapeDtype...  47.9 us

profile of v3, /device:TPU:1, one launch (start us, length us, event | category | flops | bytes accessed | tf_op | source)
XLA Modules:
  0.0 48.8 jit_solution(8580108075215794290)
XLA Ops:
  0.0 47.9 %shard_map.64 = f32[90,8,256]{2,1,0:T(8,128)S(1)} custom-call(f32[90,8,256]{2,1,0:T(8,128)} %bitcast.3, s32[8]{0:T(128)} %flag_hbm.1, s32[8]{0:T(128)} %cut_hbm.1, f32[32,16,128]{2,1,0:T(8,128)} %constant.6.clone.coef_hbm, bf16[16,384,192]{2,1,0:T(8,128)(2,1)} %constant.7.clone.table_hbm, f32[96,128]{1,0:T(8,128)} %constant.8.clone.wave_hbm), custom_call_target="tpu_custom_call" | custom-call | tf_op jit(solution)/shard_map/pallas_call | solution.py:482
  47.9 0.9 %copy.8 = f32[8,90,256]{2,0,1:T(8,128)} copy(f32[8,90,256]{2,0,1:T(8,128)S(1)} %bitcast.2) | data formatting | bytes 1474560

commit v4 on v3

--- a/solution.py
+++ b/solution.py
@@ -161,8 +161,11 @@
     def field(row, part):
         return jnp.concatenate([state[:, row, pl.ds(part * LANES, LANES)], spare], axis=0)
 
-    above = lax.rem(lat + bands - 1, bands)
-    below = lax.rem(lat + 1, bands)
+    above = jnp.maximum(lat - 1, 0)
+    below = jnp.minimum(lat + 1, bands - 1)
+    sides = (lat > 0, lat < bands - 1)
+    greeted = jnp.where(lat > 0, 1, 0) + jnp.where(lat < bands - 1, 1, 0)
+    odd = lax.rem(lat, 2)
     chip = lon // 2
     core = lon % 2
 
@@ -183,8 +186,6 @@
     barrier = pltpu.get_barrier_semaphore()
     for offset in range(1, PARTS):
         pl.semaphore_signal(barrier, inc=1, device_id=(lat, lax.rem(lon + offset, PARTS)), device_id_type=MESH)
-    pl.semaphore_signal(barrier, inc=1, device_id=(above, lon), device_id_type=MESH)
-    pl.semaphore_signal(barrier, inc=1, device_id=(below, lon), device_id_type=MESH)
 
     lane = lax.broadcasted_iota(jnp.int32, (wide, LANES), 1)
     line = lax.broadcasted_iota(jnp.int32, (wide, LANES), 0)
@@ -275,7 +276,11 @@
     def pack_and_send(pair, at, kind):
         pack(pair, 8 * at + kind)
         if pair == 1:
-            pl.semaphore_wait(barrier, PARTS + 1)
+            pl.semaphore_wait(barrier, PARTS - 1 + odd * greeted)
+            for present, device in zip(sides, (above, below)):
+                @pl.when(present)
+                def _():
+                    pl.semaphore_signal(barrier, inc=1, device_id=(device, lon), device_id_type=MESH)
         for offset in range(4):
             target = 8 * at + 2 * lax.rem(chip + offset, 4) + kind
 
@@ -303,11 +308,21 @@
         turned = pltpu.roll(field(row, 1), 64, 1)
         message = jnp.where(first, turned, winds[row + 1])
         halo_out[side] = jnp.where(line == width, cuts[pl.ds(row + 1, 1), :], message)
-    for halo in halos:
-        halo.start()
+
+    @pl.when(odd == 0)
+    def _():
+        pl.semaphore_wait(barrier, greeted)
 
     for side in range(2):
-        halos[side].wait_recv()
+        pl.when(sides[side])(halos[side].start)
+
+    for side in range(2):
+        pl.when(sides[1 - side])(halos[side].wait_recv)
+
+        @pl.when(jnp.logical_not(sides[side]))
+        def _():
+            halo_in[side] = jnp.zeros((wide, LANES), jnp.float32)
+
     inside = jnp.where(lat > 0, 0.015, 0.0)
     upper = halo_in[0]
     cuts[pl.ds(0, 1), :] = upper[width : width + 1]
@@ -416,8 +431,8 @@
         return carry
 
     lax.fori_loop(0, PARTS, pack_back, 0, unroll=PARTS)
+    send_to(backward_copy, 1)
     send_to(backward_copy, 0)
-    send_to(backward_copy, 1)
     brecv[lon] = bsend[lon]
 
     def unpack(pair, slot):
@@ -462,8 +477,8 @@
         return carry
 
     lax.fori_loop(1, PARTS, finish, 0)
-    for halo in halos:
-        halo.wait_send()
+    for side in range(2):
+        pl.when(sides[side])(halos[side].wait_send)
 
 
 def solution(mesh):

time: 48.9 us -> 44.7 us (0.914)
  the two profiles are of different devices: /device:TPU:1 before, /device:TPU:206 now
where the time goes in v4:
time: 44.7 us; the launch traced here: 44.6 us
  Pallas kernels  43.7 us (98%)
  local copies, waits for them, and re-layouts  0.87 us (2%)
    pallas_call x1, Pallas kernels, body(): pl.pallas_call(functools.partial(kernel, bands), out_shape=jax.ShapeDtype...  43.7 us

profile of v4, /device:TPU:206, one launch (start us, length us, event | category | flops | bytes accessed | tf_op | source)
XLA Modules:
  0.0 44.6 jit_solution(4312359670503648001)
XLA Ops:
  0.0 43.7 %shard_map.64 = f32[90,8,256]{2,1,0:T(8,128)S(1)} custom-call(f32[90,8,256]{2,1,0:T(8,128)} %bitcast.3, s32[8]{0:T(128)} %flag_hbm.1, s32[8]{0:T(128)} %cut_hbm.1, f32[32,16,128]{2,1,0:T(8,128)} %constant.6.clone.coef_hbm, bf16[16,384,192]{2,1,0:T(8,128)(2,1)} %constant.7.clone.table_hbm, f32[96,128]{1,0:T(8,128)} %constant.8.clone.wave_hbm), custom_call_target="tpu_custom_call" | custom-call | tf_op jit(solution)/shard_map/pallas_call | solution.py:497
  43.7 0.9 %copy.8 = f32[8,90,256]{2,0,1:T(8,128)} copy(f32[8,90,256]{2,0,1:T(8,128)S(1)} %bitcast.2) | data formatting | bytes 1474560

commit v5 on v4

--- a/solution.py
+++ b/solution.py
@@ -13,6 +13,7 @@
 PARTS = 16
 LANES = 128
 OPEN_CUT = 4096.0
+DEPTH = 8
 PACKED = 72
 
 
@@ -150,7 +151,7 @@
     result,
     state, flag_ref, cut_ref, winds, press, slopes, cuts, coef, table, waves, damps, turns,
     halo_out, halo_in, send, recv, spectra, fields, bsend, brecv,
-    load_sem, halo_send, halo_recv, send_sem, recv_sem, bsend_sem, brecv_sem,
+    hello, load_sem, halo_send, halo_recv, send_sem, recv_sem, bsend_sem, brecv_sem,
 ):
     lat = lax.axis_index("lat")
     lon = lax.axis_index("lon")
@@ -164,8 +165,11 @@
     above = jnp.maximum(lat - 1, 0)
     below = jnp.minimum(lat + 1, bands - 1)
     sides = (lat > 0, lat < bands - 1)
-    greeted = jnp.where(lat > 0, 1, 0) + jnp.where(lat < bands - 1, 1, 0)
-    odd = lax.rem(lat, 2)
+    place = lax.rem(lat, DEPTH)
+    paired = (place != 0, place != DEPTH - 1)
+    opening = (place == 0) & sides[0]
+    closing = (place == DEPTH - 1) & sides[1]
+    known = jnp.where(paired[0], 1, 0) + jnp.where(sides[1], 1, 0)
     chip = lon // 2
     core = lon % 2
 
@@ -186,6 +190,11 @@
     barrier = pltpu.get_barrier_semaphore()
     for offset in range(1, PARTS):
         pl.semaphore_signal(barrier, inc=1, device_id=(lat, lax.rem(lon + offset, PARTS)), device_id_type=MESH)
+
+    for side, device in ((0, above), (1, below)):
+        @pl.when(paired[side])
+        def _():
+            pl.semaphore_signal(barrier, inc=1, device_id=(device, lon), device_id_type=MESH)
 
     lane = lax.broadcasted_iota(jnp.int32, (wide, LANES), 1)
     line = lax.broadcasted_iota(jnp.int32, (wide, LANES), 0)
@@ -227,20 +236,20 @@
             for at in range(4):
                 if at != quarter:
                     chunk = jnp.where(block == at, pltpu.roll(sources[at], (16 * (at - quarter)) % LANES, 1), chunk)
-            send[slot + 2 * quarter] = chunk
-
-    halos = []
-    for side, device in ((0, above), (1, below)):
-        halos.append(
-            pltpu.make_async_remote_copy(
-                src_ref=halo_out.at[side],
-                dst_ref=halo_in.at[1 - side],
-                send_sem=halo_send.at[side],
-                recv_sem=halo_recv.at[1 - side],
-                device_id=(device, lon),
-                device_id_type=MESH,
-            )
+            send[slot + 4 * quarter] = chunk
+
+    def halo_copy(side, slot, device):
+        return pltpu.make_async_remote_copy(
+            src_ref=halo_out.at[side],
+            dst_ref=halo_in.at[slot],
+            send_sem=halo_send.at[side],
+            recv_sem=halo_recv.at[slot],
+            device_id=(device, lon),
+            device_id_type=MESH,
         )
+
+    halos = [halo_copy(0, 1, above), halo_copy(1, 0, below)]
+
     def forward_copy(source, slot, device):
         return pltpu.make_async_remote_copy(
             src_ref=send.at[source],
@@ -274,32 +283,18 @@
                     copy(target, lon, target).start()
 
     def pack_and_send(pair, at, kind):
-        pack(pair, 8 * at + kind)
-        if pair == 1:
-            pl.semaphore_wait(barrier, PARTS - 1 + odd * greeted)
-            for present, device in zip(sides, (above, below)):
-                @pl.when(present)
-                def _():
-                    pl.semaphore_signal(barrier, inc=1, device_id=(device, lon), device_id_type=MESH)
-        for offset in range(4):
-            target = 8 * at + 2 * lax.rem(chip + offset, 4) + kind
+        pack(pair, 2 * at + kind)
+        for offset in (2, 1, 3, 0):
+            target = 2 * at + 4 * lax.rem(chip // 2 + offset, 4) + kind
 
             @pl.when(target != lon)
             def _():
                 forward_copy(target, lon, target).start()
 
-    for row in range(1, 5):
-        prepare(row)
-    pack_and_send(1, 0, 0)
-    for row in range(5, 7):
-        prepare(row)
-    pack_and_send(2, 1, 0)
     prepare(0)
     prepare(rows - 1)
     for load in loads[3:5]:
         load.wait()
-    for load in loads[5:]:
-        load.start()
     for row in range(rows):
         kept = jnp.full((1, LANES), cut_ref[row], jnp.int32).astype(jnp.float32)
         flag = jnp.full((1, LANES), flag_ref[row], jnp.int32)
@@ -308,37 +303,59 @@
         turned = pltpu.roll(field(row, 1), 64, 1)
         message = jnp.where(first, turned, winds[row + 1])
         halo_out[side] = jnp.where(line == width, cuts[pl.ds(row + 1, 1), :], message)
-
-    @pl.when(odd == 0)
+    for row in range(1, 5):
+        prepare(row)
+
+    pl.semaphore_wait(barrier, PARTS - 1 + known)
+    pl.when(paired[0])(halos[0].start)
+    pl.when(sides[1])(halos[1].start)
+
+    @pl.when(opening)
     def _():
-        pl.semaphore_wait(barrier, greeted)
-
-    for side in range(2):
-        pl.when(sides[side])(halos[side].start)
-
-    for side in range(2):
-        pl.when(sides[1 - side])(halos[side].wait_recv)
-
-        @pl.when(jnp.logical_not(sides[side]))
+        pl.semaphore_signal(barrier, inc=1, device_id=(above, lon), device_id_type=MESH)
+
+    @pl.when(closing)
+    def _():
+        pl.semaphore_signal(hello.at[0], inc=1, device_id=(below, lon), device_id_type=MESH)
+
+    pack_and_send(1, 0, 0)
+    for load in loads[5:]:
+        load.start()
+    for row in range(5, 7):
+        prepare(row)
+    pack_and_send(2, 1, 0)
+
+    flip = jnp.where((place == 0) | (place == DEPTH - 1), 1, 0)
+    for step in range(2):
+        side = flip if step == 0 else 1 - flip
+        present = jnp.where(side == 0, lat, bands - 1 - lat) > 0
+
+        @pl.when(present)
+        def _():
+            halo_copy(1 - side, side, above).wait_recv()
+
+        @pl.when(jnp.logical_not(present))
         def _():
             halo_in[side] = jnp.zeros((wide, LANES), jnp.float32)
 
-    inside = jnp.where(lat > 0, 0.015, 0.0)
-    upper = halo_in[0]
-    cuts[pl.ds(0, 1), :] = upper[width : width + 1]
-    winds[0] = jnp.where(line < width, upper - 0.015 * field(0, 1), 0.0)
-    winds[1] = winds[1] + jnp.where(first | (line >= width), 0.0, inside * pltpu.roll(upper, 64, 1))
-    inside = jnp.where(lat < bands - 1, 0.015, 0.0)
-    lower = halo_in[1]
-    cuts[pl.ds(rows + 1, 1), :] = lower[width : width + 1]
-    winds[rows + 1] = jnp.where(line < width, lower + 0.015 * field(rows - 1, 1), 0.0)
-    winds[rows] = winds[rows] - jnp.where(first | (line >= width), 0.0, inside * pltpu.roll(lower, 64, 1))
-
-    pack_and_send(0, 0, 1)
-    pack_and_send(3, 1, 1)
+        outer = jnp.where(side == 0, 0, rows + 1)
+        inner = jnp.where(side == 0, 1, rows)
+        slope = jnp.where(side == 0, 0.015, -0.015)
+        inside = jnp.where(present, slope, 0.0)
+        arrived = halo_in[side]
+        cuts[pl.ds(outer, 1), :] = arrived[width : width + 1]
+        winds[outer] = jnp.where(line < width, arrived - slope * pltpu.roll(halo_out[side], 64, 1), 0.0)
+        winds[inner] = winds[inner] + jnp.where(first | (line >= width), 0.0, inside * pltpu.roll(arrived, 64, 1))
+        pack_and_send(3 * side, side, 1)
+        if step == 0:
+            @pl.when(opening)
+            def _():
+                pl.semaphore_wait(hello.at[0], 1)
+                halos[0].start()
+
     recv[lon] = send[lon]
 
-    half = chip // 4
+    half = chip % 2
     mine = (1 - core) * (1 + half) + core * 3 * half
     lanes = lax.broadcasted_iota(jnp.int32, (1, LANES), 1) // 16
     cut_even = cuts[pl.ds(2 * mine + 1, 1), :]
@@ -438,7 +455,7 @@
     def unpack(pair, slot):
         chunks = []
         for quarter in range(4):
-            source = slot + 2 * quarter
+            source = slot + 4 * quarter
 
             @pl.when(source != lon)
             def _():
@@ -466,9 +483,9 @@
         result[:, even + 1, spans] = jnp.where(first[:width], result[:, even + 1, spans], parts[3][:width])
 
     for at in range(2):
-        unpack(1 + at, 8 * at)
+        unpack(1 + at, 2 * at)
     for at in range(2):
-        unpack(3 * at, 8 * at + 1)
+        unpack(3 * at, 2 * at + 1)
 
     def finish(offset, carry):
         target = lax.rem(lon + offset, PARTS)
@@ -520,6 +537,7 @@
                 pltpu.VMEM((8, 2 * wide, LANES), f32),
                 pltpu.VMEM((PARTS, PACKED, LANES), f32),
                 pltpu.VMEM((PARTS, PACKED, LANES), f32),
+                pltpu.SemaphoreType.REGULAR((1,)),
                 dma((7,)),
                 dma((2,)),
                 dma((2,)),

time: 44.7 us -> 43.9 us (0.982)
  the two profiles are of different devices: /device:TPU:206 before, /device:TPU:8 now
where the time goes in v5:
time: 43.9 us; the launch traced here: 43.8 us
  Pallas kernels  42.9 us (98%)
  local copies, waits for them, and re-layouts  0.87 us (2%)
    pallas_call x1, Pallas kernels, body(): pl.pallas_call(functools.partial(kernel, bands), out_shape=jax.ShapeDtype...  42.9 us

profile of v5, /device:TPU:8, one launch (start us, length us, event | category | flops | bytes accessed | tf_op | source)
XLA Modules:
  0.0 43.8 jit_solution(13114108497498530232)
XLA Ops:
  0.0 42.9 %shard_map.64 = f32[90,8,256]{2,1,0:T(8,128)S(1)} custom-call(f32[90,8,256]{2,1,0:T(8,128)} %bitcast.3, s32[8]{0:T(128)} %flag_hbm.1, s32[8]{0:T(128)} %cut_hbm.1, f32[32,16,128]{2,1,0:T(8,128)} %constant.6.clone.coef_hbm, bf16[16,384,192]{2,1,0:T(8,128)(2,1)} %constant.7.clone.table_hbm, f32[96,128]{1,0:T(8,128)} %constant.8.clone.wave_hbm), custom_call_target="tpu_custom_call" | custom-call | tf_op jit(solution)/shard_map/pallas_call | solution.py:514
  42.9 0.9 %copy.8 = f32[8,90,256]{2,0,1:T(8,128)} copy(f32[8,90,256]{2,0,1:T(8,128)S(1)} %bitcast.2) | data formatting | bytes 1474560

commit v6 on v5

--- a/solution.py
+++ b/solution.py
@@ -449,7 +449,14 @@
 
     lax.fori_loop(0, PARTS, pack_back, 0, unroll=PARTS)
     send_to(backward_copy, 1)
-    send_to(backward_copy, 0)
+    for turn in (1, 0):
+        for offset in (2, 1, 3, 0):
+            target = 4 * lax.rem(chip // 2 + offset, 4) + 2 * turn
+
+            @pl.when(target != lon)
+            def _():
+                backward_copy(target, lon, target).start()
+
     brecv[lon] = bsend[lon]
 
     def unpack(pair, slot):

time: 43.9 us -> 43.5 us (level)
  the two profiles are of different devices: /device:TPU:8 before, /device:TPU:16 now
where the time goes in v6:
time: 43.5 us; the launch traced here: 43.4 us
  Pallas kernels  42.5 us (98%)
  local copies, waits for them, and re-layouts  0.87 us (2%)
    pallas_call x1, Pallas kernels, body(): pl.pallas_call(functools.partial(kernel, bands), out_shape=jax.ShapeDtype...  42.5 us

profile of v6, /device:TPU:16, one launch (start us, length us, event | category | flops | bytes accessed | tf_op | source)
XLA Modules:
  0.0 43.4 jit_solution(6563558406799081495)
XLA Ops:
  0.0 42.5 %shard_map.64 = f32[90,8,256]{2,1,0:T(8,128)S(1)} custom-call(f32[90,8,256]{2,1,0:T(8,128)} %bitcast.3, s32[8]{0:T(128)} %flag_hbm.1, s32[8]{0:T(128)} %cut_hbm.1, f32[32,16,128]{2,1,0:T(8,128)} %constant.6.clone.coef_hbm, bf16[16,384,192]{2,1,0:T(8,128)(2,1)} %constant.7.clone.table_hbm, f32[96,128]{1,0:T(8,128)} %constant.8.clone.wave_hbm), custom_call_target="tpu_custom_call" | custom-call | tf_op jit(solution)/shard_map/pallas_call | solution.py:521
  42.5 0.9 %copy.8 = f32[8,90,256]{2,0,1:T(8,128)} copy(f32[8,90,256]{2,0,1:T(8,128)S(1)} %bitcast.2) | data formatting | bytes 1474560

commit v7 on v6

--- a/solution.py
+++ b/solution.py
@@ -449,9 +449,12 @@
 
     lax.fori_loop(0, PARTS, pack_back, 0, unroll=PARTS)
     send_to(backward_copy, 1)
-    for turn in (1, 0):
-        for offset in (2, 1, 3, 0):
-            target = 4 * lax.rem(chip // 2 + offset, 4) + 2 * turn
+    for turn, offsets in ((1, (2, 1, 3, 0)), (2, (1, 0)), (0, (1, 0))):
+        for offset in offsets:
+            if turn == 1:
+                target = 4 * lax.rem(chip // 2 + offset, 4) + 2
+            else:
+                target = 8 * lax.rem(chip // 4 + offset, 2) + 2 * turn
 
             @pl.when(target != lon)
             def _():

time: 43.5 us -> 43.3 us (level)
  no operation moved by 1% of the time
where the time goes in v7:
time: 43.3 us; the launch traced here: 43.2 us
  Pallas kernels  42.3 us (98%)
  local copies, waits for them, and re-layouts  0.87 us (2%)
    pallas_call x1, Pallas kernels, body(): pl.pallas_call(functools.partial(kernel, bands), out_shape=jax.ShapeDtype...  42.3 us

profile of v7, /device:TPU:16, one launch (start us, length us, event | category | flops | bytes accessed | tf_op | source)
XLA Modules:
  0.0 43.2 jit_solution(8321789834145443271)
XLA Ops:
  0.0 42.3 %shard_map.64 = f32[90,8,256]{2,1,0:T(8,128)S(1)} custom-call(f32[90,8,256]{2,1,0:T(8,128)} %bitcast.3, s32[8]{0:T(128)} %flag_hbm.1, s32[8]{0:T(128)} %cut_hbm.1, f32[32,16,128]{2,1,0:T(8,128)} %constant.6.clone.coef_hbm, bf16[16,384,192]{2,1,0:T(8,128)(2,1)} %constant.7.clone.table_hbm, f32[96,128]{1,0:T(8,128)} %constant.8.clone.wave_hbm), custom_call_target="tpu_custom_call" | custom-call | tf_op jit(solution)/shard_map/pallas_call | solution.py:524
  42.3 0.9 %copy.8 = f32[8,90,256]{2,0,1:T(8,128)} copy(f32[8,90,256]{2,0,1:T(8,128)S(1)} %bitcast.2) | data formatting | bytes 1474560

commit v8 on v6

--- a/solution.py
+++ b/solution.py
@@ -448,10 +448,9 @@
         return carry
 
     lax.fori_loop(0, PARTS, pack_back, 0, unroll=PARTS)
-    send_to(backward_copy, 1)
-    for turn in (1, 0):
+    for turn, kind in ((0, 1), (1, 1), (1, 0), (0, 0)):
         for offset in (2, 1, 3, 0):
-            target = 4 * lax.rem(chip // 2 + offset, 4) + 2 * turn
+            target = 4 * lax.rem(chip // 2 + offset, 4) + 2 * turn + kind
 
             @pl.when(target != lon)
             def _():

time: 43.5 us -> 43.5 us (level)
  no operation moved by 1% of the time
where the time goes in v8:
time: 43.5 us; the launch traced here: 43.4 us
  Pallas kernels  42.5 us (98%)
  local copies, waits for them, and re-layouts  0.87 us (2%)
    pallas_call x1, Pallas kernels, body(): pl.pallas_call(functools.partial(kernel, bands), out_shape=jax.ShapeDtype...  42.5 us

profile of v8, /device:TPU:16, one launch (start us, length us, event | category | flops | bytes accessed | tf_op | source)
XLA Modules:
  0.0 43.4 jit_solution(16634073830401113622)
XLA Ops:
  0.0 42.5 %shard_map.64 = f32[90,8,256]{2,1,0:T(8,128)S(1)} custom-call(f32[90,8,256]{2,1,0:T(8,128)} %bitcast.3, s32[8]{0:T(128)} %flag_hbm.1, s32[8]{0:T(128)} %cut_hbm.1, f32[32,16,128]{2,1,0:T(8,128)} %constant.6.clone.coef_hbm, bf16[16,384,192]{2,1,0:T(8,128)(2,1)} %constant.7.clone.table_hbm, f32[96,128]{1,0:T(8,128)} %constant.8.clone.wave_hbm), custom_call_target="tpu_custom_call" | custom-call | tf_op jit(solution)/shard_map/pallas_call | solution.py:520
  42.5 0.9 %copy.8 = f32[8,90,256]{2,0,1:T(8,128)} copy(f32[8,90,256]{2,0,1:T(8,128)S(1)} %bitcast.2) | data formatting | bytes 1474560
